TPU v7x, 512 devices: a whole 4x8x8 slice. The times are simulated.
512 devices in a mesh: row: 16 (over x, z_hi), col: 32 (over z_lo, y, core).
Axes of the slice: x: 4, y: 8, z: 8 (z_hi: 4, z_lo: 2; z = z_hi * 2 + z_lo), core: 2. Of those that a mesh axis runs over, the one named last changes fastest.
Arguments:
- bin_features: bfloat16 [4096, 512], P('row'), may hold values from -6 to 6
- w_left: bfloat16 [512, 32], replicated, may hold values from -0.25 to 0.25
- w_right: bfloat16 [512, 32], replicated, may hold values from -0.25 to 0.25
- depth_kernel: float32 [9, 32], replicated, may hold values from -2 to 2
- w_point: bfloat16 [32, 32], replicated, may hold values from -1 to 1
- w_head: bfloat16 [32, 24], replicated, may hold values from -1 to 1
- cotangent: bfloat16 [24, 4096, 4096], P(None, 'row', 'col'), may hold values from -6 to 6
Outputs:
- grad_features: bfloat16 [4096, 512], P('row')
- grad_w_left: float32 [512, 32], replicated
- grad_w_right: float32 [512, 32], replicated
- grad_kernel: float32 [9, 32], replicated
- grad_point: float32 [32, 32], replicated
- grad_head: float32 [32, 24], replicated
All inputs are finite; a program needn't handle non-finite values.
Results may differ from a plain program's by a relative error of at most 0.019.
Values may be sent and summed in bfloat16 or wider, within the bound.
No kernel may reach another device: no remote copies, remote signals or barrier semaphores. Data moves between devices by JAX's collectives and lax.ppermute only.
A program may use at most 64 MiB of HBM per device.

v0:
```python
import math
import jax
import jax.numpy as jnp
from jax import lax
from jax.sharding import PartitionSpec as P

DILATION_STEP = 4


def from_root(block, axis, source):
    block = jnp.where(lax.axis_index(axis) == source, block, jnp.zeros_like(block))
    return lax.psum(block, axis)


def extended(x, sides, width):
    for axis, dim in sides:
        count, length = (lax.axis_size(axis), x.shape[dim])
        up = [(i, (i + 1) % count) for i in range(count - 1)]
        down = [(j, i) for i, j in up]
        last = lax.slice_in_dim(x, length - width, length, axis=dim)
        first = lax.slice_in_dim(x, 0, width, axis=dim)
        before = lax.ppermute(last, axis, up)
        after = lax.ppermute(first, axis, down)
        x = jnp.concatenate([before, x, after], axis=dim)
    return x


def silu_slope(values):
    logistic = jax.nn.sigmoid(values)
    return logistic * (1.0 + values * (1.0 - logistic))


def depthwise(kernel_taps, padded, output_rows, output_columns):
    result = jnp.zeros((padded.shape[0], output_rows, output_columns), jnp.float32)
    for kernel_tap_row in range(3):
        for kernel_tap_column in range(3):
            result = result + kernel_taps[3 * kernel_tap_row + kernel_tap_column][
                :, None, None
            ] * padded[
                :,
                DILATION_STEP * kernel_tap_row : DILATION_STEP * kernel_tap_row + output_rows,
                DILATION_STEP * kernel_tap_column : DILATION_STEP * kernel_tap_column
                + output_columns,
            ].astype(
                jnp.float32
            )
    return result


def body(bin_features, w_left, w_right, depth_kernel, w_point, w_head, cotangent):
    rows_per_tile = bin_features.shape[0]
    columns_per_tile = cotangent.shape[2]
    chans = w_left.shape[1]
    row_count = lax.axis_size("row")
    col_count = lax.axis_size("col")
    panel_ratio = col_count // row_count
    contact_map_bins = rows_per_tile * row_count
    grad_scale = 1.0 / math.sqrt(contact_map_bins)
    row_index = lax.axis_index("row")
    col_index = lax.axis_index("col")
    left_panel = jnp.dot(bin_features, w_left, preferred_element_type=jnp.float32).astype(
        jnp.bfloat16
    )
    offset = col_index % panel_ratio * columns_per_tile
    own_rows = lax.dynamic_slice_in_dim(bin_features, offset, columns_per_tile, 0)
    right_own = jnp.dot(own_rows, w_right, preferred_element_type=jnp.float32).astype(jnp.bfloat16)
    right_panel = from_root(right_own, "row", col_index // panel_ratio)
    pair_matrix = (
        left_panel.astype(jnp.float32).T[:, :, None] + right_panel.astype(jnp.float32).T[:, None, :]
    ).astype(jnp.bfloat16)
    extended_pair = extended(pair_matrix, (("row", 1), ("col", 2)), DILATION_STEP)
    convolved_map = depthwise(depth_kernel, extended_pair, rows_per_tile, columns_per_tile)
    trunk_gradient = (
        grad_scale
        * jnp.einsum("ch,hij->cij", w_head, cotangent, preferred_element_type=jnp.float32)
    ).astype(jnp.bfloat16)
    grad_hidden = jnp.einsum(
        "co,oij->cij", w_point, trunk_gradient, preferred_element_type=jnp.float32
    )
    convolved_gradient = (grad_hidden * silu_slope(convolved_map)).astype(jnp.bfloat16)
    extended_gradient = extended(convolved_gradient, (("row", 1), ("col", 2)), DILATION_STEP)
    hidden_state = jax.nn.silu(convolved_map).astype(jnp.bfloat16)
    mixed_out = jnp.einsum("co,cij->oij", w_point, hidden_state, preferred_element_type=jnp.float32)
    centre_offset = extended_pair[
        :,
        DILATION_STEP : DILATION_STEP + rows_per_tile,
        DILATION_STEP : DILATION_STEP + columns_per_tile,
    ]
    trunk_matrix = (centre_offset.astype(jnp.float32) + mixed_out).astype(jnp.bfloat16)
    conv_f32 = convolved_gradient.astype(jnp.float32)
    backward_pass = jnp.zeros((chans, rows_per_tile, columns_per_tile), jnp.float32)
    kern_terms = []
    for kernel_tap_row in range(3):
        for kernel_tap_column in range(3):
            backward_pass = backward_pass + depth_kernel[3 * kernel_tap_row + kernel_tap_column][
                :, None, None
            ] * extended_gradient[
                :,
                DILATION_STEP * (2 - kernel_tap_row) : DILATION_STEP * (2 - kernel_tap_row)
                + rows_per_tile,
                DILATION_STEP * (2 - kernel_tap_column) : DILATION_STEP * (2 - kernel_tap_column)
                + columns_per_tile,
            ].astype(
                jnp.float32
            )
            shifted_window = extended_pair[
                :,
                DILATION_STEP * kernel_tap_row : DILATION_STEP * kernel_tap_row + rows_per_tile,
                DILATION_STEP * kernel_tap_column : DILATION_STEP * kernel_tap_column
                + columns_per_tile,
            ].astype(jnp.float32)
            kern_terms.append(jnp.sum(conv_f32 * shifted_window, axis=(1, 2)))
    kernel_part = jnp.stack(kern_terms)
    pair_gradient = trunk_gradient.astype(jnp.float32) + backward_pass
    left_part = jnp.sum(pair_gradient, axis=2).T
    right_part = jnp.sum(pair_gradient, axis=1).T
    point_part = jnp.einsum(
        "fsk,gsk->fg", hidden_state, trunk_gradient, preferred_element_type=jnp.float32
    )
    head_part = jnp.einsum(
        "ydq,gdq->yg", trunk_matrix, cotangent, preferred_element_type=jnp.float32
    )
    grad_left = lax.psum(left_part, "col").astype(jnp.bfloat16)
    column_total = lax.psum(right_part, "row").astype(jnp.bfloat16)
    all_panels = lax.all_gather(column_total, "col", axis=0, tiled=True)
    grad_right = lax.dynamic_slice_in_dim(all_panels, row_index * rows_per_tile, rows_per_tile, 0)
    grad_features = (
        jnp.dot(grad_left, w_left.T, preferred_element_type=jnp.float32)
        + jnp.dot(grad_right, w_right.T, preferred_element_type=jnp.float32)
    ).astype(jnp.bfloat16)
    contract = (((0,), (0,)), ((), ()))
    wleft_part = lax.dot_general(
        bin_features, grad_left, contract, preferred_element_type=jnp.float32
    )
    wright_part = lax.dot_general(
        bin_features, grad_right, contract, preferred_element_type=jnp.float32
    )
    kernel_sum, point_sum, head_sum = lax.psum((kernel_part, point_part, head_part), ("row", "col"))
    wleft_sum, wright_sum = lax.psum((wleft_part, wright_part), "row")
    return (
        grad_features,
        grad_scale * wleft_sum,
        grad_scale * wright_sum,
        grad_scale * kernel_sum,
        grad_scale * point_sum,
        grad_scale * head_sum,
    )


def solution(mesh):
    placed = (P("row", None), P(), P(), P(), P(), P(), P(None, "row", "col"))
    return jax.shard_map(
        body,
        mesh=mesh,
        in_specs=placed,
        out_specs=(P("row", None), P(), P(), P(), P(), P()),
        check_vma=False,
    )
```

profile of v0, /device:TPU:8, one launch (start us, length us, event | category | flops | bytes accessed | tf_op | source)
XLA Modules:
  0.0 674.3 jit_solution(18254187634809960480)
XLA Ops:
  7.3 1.1 fusion.34
  8.4 50.8 %psum.56 = bf16[32,128]{1,0:T(8,128)(2,1)S(1)} all-reduce(bf16[32,128]{1,0:T(8,128)(2,1)S(1)} %fusion.34), channel_id=1, replica_groups=mesh['row'=16,'col'=32] {'row'}, use_global_device_ids=true, to_apply=%region_0.1 | all-reduce | flops 4096 | bytes 16384 | tf_op jit(solution)/shard_map/psum | solution.py:12
  59.2 1.1 fusion.29
  60.5 1.7 add_convert_fusion
  62.2 1.3 collective-permute-start
  63.5 1.3 collective-permute-start.1
  64.8 3.5 multiply_convert_fusion.1
  68.3 1.9 collective-permute-done.1
  70.5 2.9 fusion.51
  73.5 3.6 copy.20
  77.1 3.6 copy.22
  80.8 1.9 collective-permute-start.3
  82.7 2.6 collective-permute-start.2
  85.3 3.3 collective-permute-done.2
  88.6 3.0 copy.21
  91.6 3.0 copy.23
  94.7 7.2 %maximum_maximum_fusion = (bf16[32,264,132]{2,0,1:T(8,128)(2,1)S(1)}, bf16[32,264,132]{2,0,1:T(8,128)(2,1)S(1)}) fusion(bf16[32,4,128]{2,0,1:T(8,128)(2,1)S(1)} %collective-permute-done.1, bf16[32,256,128]{2,0,1:T(8,128)(2,1)} %copy-done.1, bf16[32,4,128]{2,0,1:T(8,128)(2,1)S(1)} %collective-permute-done, bf16[32,264,4]{2,0,1:T(8,128)(2,1)} %copy.21, ...), kind=kLoop, calls=%fused_computation.20 | loop fusion | flops 17842176 | bytes 6758400 | tf_op jit(solution)/shard_map/concatenate | solution.py:24
  101.9 10.2 %multiply_convert_fusion = (bf16[32,256,128]{2,0,1:T(8,128)(2,1)}, f32[32,256,128]{2,0,1:T(8,128)}) fusion(bf16[32,264,132]{2,0,1:T(8,128)(2,1)S(1)} %get-tuple-element.34, f32[32]{0:T(128)S(1)} %get-tuple-element.48, bf16[32,4,128]{2,0,1:T(8,128)(2,1)S(1)} %collective-permute-done.1, bf16[32,256,128]{2,0,1:T(8,128)(2,1)S(1)} %copy-done.2, ...), kind=kLoop, calls=%fused_computation.50 | loop fusion | flops 36700160 | bytes 21087360 | tf_op jit(solution)/shard_map/convert_element_type | solution.py:82
  112.1 3.4 fusion.30
  115.6 3.0 convolution_bitcast_fusion.2
  119.0 13.2 %fusion.23 = (f32[32]{0:T(128)S(1)}, f32[32]{0:T(128)S(1)}, f32[32]{0:T(128)S(1)}, f32[32]{0:T(128)S(1)}, f32[32]{0:T(128)S(1)}, /*index=5*/f32[32]{0:T(128)S(1)...) fusion(bf16[32,264,132]{2,0,1:T(8,128)(2,1)} %copy-done.5, ...), kind=kOutput, calls=%fused_computation.47 | convolution fusion | flops 110100192 | bytes 23186560 | tf_op jit(solution)/shard_map/co,oij->cij/dot_general | solution.py:77
  132.3 96.0 %all-reduce = (f32[9,32]{1,0:T(8,128)S(1)}, f32[32,32]{1,0:T(8,128)S(1)}, f32[32,24]{0,1:T(8,128)S(1)}) all-reduce(f32[9,32]{1,0:T(8,128)S(1)} %stack.39, f32[32,32]{1,0:T(8,128)S(1)} %convolution_bitcast_fusion.2, f32[32,24]{0,1:T(8,128)S(1)} %fusion.30), channel_id=1, replica_groups=mesh['row'=16,'col'=32] {'row','col'}, use_global_device_ids=true, to_apply=%region_16.17 | all-reduce | flops 2080 | bytes 16640 | tf_op jit(solution)/shard_map/psum | solution.py:138
  228.3 0.6 broadcast_multiply_fusion.2
  228.9 0.8 fusion.52
  229.7 2.8 collective-permute-start.4
  232.5 1.5 collective-permute-start.5
  234.0 0.6 broadcast_multiply_fusion.3
  234.6 5.1 collective-permute-done.5
  239.7 1.9 pad_maximum_fusion.3
  241.5 2.9 fusion.50
  244.5 3.6 copy.24
  248.1 3.6 copy.26
  251.8 1.9 collective-permute-start.7
  253.7 3.6 collective-permute-start.6
  257.3 0.6 broadcast_multiply_fusion.4
  257.9 1.6 collective-permute-done.6
  259.5 3.0 copy.25
  262.6 3.0 copy.27
  265.6 7.2 %pad_maximum_fusion.1 = (bf16[32,264,132]{2,0,1:T(8,128)(2,1)S(1)}, bf16[32,264,132]{2,0,1:T(8,128)(2,1)S(1)}) fusion(bf16[32,264,4]{2,0,1:T(8,128)(2,1)} %copy.25, bf16[32,4,128]{2,0,1:T(8,128)(2,1)S(1)} %collective-permute-done.5, bf16[32,256,128]{2,0,1:T(8,128)(2,1)} %get-tuple-element.50, bf16[32,4,128]{2,0,1:T(8,128)(2,1)S(1)} %collective-permute-done.4, ...), kind=kLoop, calls=%fused_computation.22 | loop fusion | flops 17842176 | bytes 6758400 | tf_op jit(solution)/shard_map/concatenate | solution.py:24
  272.9 7.2 %fusion.48 = (f32[32,128]{1,0:T(8,128)S(1)}, f32[32,256]{0,1:T(8,128)S(1)}) fusion(bf16[32,264,132]{2,0,1:T(8,128)(2,1)S(1)} %get-tuple-element.30, f32[32]{0:T(128)S(1)} %get-tuple-element.48, bf16[32,256,128]{2,0,1:T(8,128)(2,1)S(1)} %copy-done.6, bf16[32,4,128]{2,0,1:T(8,128)(2,1)S(1)} %collective-permute-done.4, f32[32]{0:T(128)S(1)} %get-tuple-element.49, ...), kind=kLoop, calls=%fused_computation.100 | loop fusion | flops 33542144 | bytes 16893056 | tf_op jit(solution)/shard_map/reduce_sum | solution.py:116
  280.2 102.3 %psum.57 = bf16[256,32]{1,0:T(8,128)(2,1)S(1)} all-reduce(f32[256,32]{1,0:T(8,128)S(1)} %bitcast.73), channel_id=1, replica_groups=mesh['row'=16,'col'=32] {'col'}, use_global_device_ids=true, to_apply=%region_2.3 | all-reduce | flops 8192 | bytes 49152 | tf_op jit(solution)/shard_map/psum | solution.py:123
  382.4 0.8 convolution_bitcast_fusion.1
  383.5 80.7 %psum.58 = bf16[128,32]{0,1:T(8,128)(2,1)S(1)} all-reduce(f32[128,32]{0,1:T(8,128)S(1)} %bitcast.74), channel_id=1, replica_groups=mesh['row'=16,'col'=32] {'row'}, use_global_device_ids=true, to_apply=%region_4.5 | all-reduce | flops 4096 | bytes 24576 | tf_op jit(solution)/shard_map/psum | solution.py:124
  464.2 35.4 %all_gather.3 = bf16[4096,32]{0,1:T(8,128)(2,1)S(1)} all-gather(bf16[128,32]{0,1:T(8,128)(2,1)S(1)} %psum.58), channel_id=1, replica_groups=mesh['row'=16,'col'=32] {'col'}, dimensions={0}, use_global_device_ids=true | all-gather | bytes 270336 | tf_op jit(solution)/shard_map/all_gather | solution.py:125
  499.6 0.8 convolution_bitcast_fusion
  500.4 1.0 fusion.28
  501.3 164.6 %all-reduce.4.cloned.1.call-done = (f32[512,32]{0,1:T(8,128)}, f32[512,32]{0,1:T(8,128)}) async-done(((f32[512,32]{0,1:T(8,128)}, f32[512,32]{0,1:T(8,128)}), (f32[512,32]{0,1:T(8,128)}, f32[512,32]{0,1:T(8,128)})) %all-reduce.4.cloned.1.call-update) | async-done | bytes 131088 | tf_op jit(solution)/shard_map/psum | solution.py:139
  665.9 1.5 broadcast_multiply_fusion
  (41 shorter events, 1.2 us)
Async XLA Ops:
  7.2 57.7 %copy-start = (bf16[24,256,128]{2,1,0:T(8,128)(2,1)S(1)}, bf16[24,256,128]{2,1,0:T(8,128)(2,1)}, u32[]{:S(2)}) copy-start(bf16[24,256,128]{2,1,0:T(8,128)(2,1)} %param.13) | copy-start | bytes 4718596
  7.2 658.8 %all-reduce.4.cloned.1.call-start = ((), (), s32[]{:S(2)}) async-start(), calls=%async_computation | async-start | bytes 262144 | tf_op jit(solution)/shard_map/psum | solution.py:139
  62.2 8.0 %copy-start.1 = (bf16[32,256,128]{2,0,1:T(8,128)(2,1)}, bf16[32,256,128]{2,0,1:T(8,128)(2,1)S(1)}, u32[]{:S(2)}) copy-start(bf16[32,256,128]{2,0,1:T(8,128)(2,1)S(1)} %add_convert_fusion) | copy-start | bytes 6291460
  62.2 6.1 collective-permute-start
  63.5 6.7 collective-permute-start.1
  73.5 11.8 %copy-start.12 = (f32[9,32]{1,0:T(8,128)S(1)}, f32[9,32]{1,0:T(8,128)}, u32[]{:S(2)}) copy-start(f32[9,32]{1,0:T(8,128)} %param.10) | copy-start | bytes 3460
  80.8 10.9 %collective-permute-start.3 = (bf16[32,264,4]{1,0,2:T(8,128)(2,1)S(1)}, bf16[32,264,4]{1,0,2:T(8,128)(2,1)S(1)}, u32[]{:S(2)}, u32[]{:S(2)}) collective-permute-start(bf16[32,264,4]{1,0,2:T(8,128)(2,1)S(1)} %copy.22), channel_id=1, source_target_pairs={{1,0},{2,1},{3,2},{4,3},{5,4},{6,5},{7,6},{8,7},{9,8},{10,9},{11,1... | collective-permute-start | bytes 202760 | tf_op jit(solution)/shard_map/ppermute | solution.py:23
  82.7 5.9 collective-permute-start.2
  94.7 7.2 %copy-start.2 = (bf16[32,256,128]{2,0,1:T(8,128)(2,1)S(1)}, bf16[32,256,128]{2,0,1:T(8,128)(2,1)}, u32[]{:S(2)}) copy-start(bf16[32,256,128]{2,0,1:T(8,128)(2,1)} %copy-done.1) | copy-start | bytes 6291460
  101.9 10.2 %copy-start.4 = (bf16[32,264,132]{2,0,1:T(8,128)(2,1)}, bf16[32,264,132]{2,0,1:T(8,128)(2,1)S(1)}, u32[]{:S(2)}) copy-start(bf16[32,264,132]{2,0,1:T(8,128)(2,1)S(1)} %get-tuple-element.33) | copy-start | bytes 6690820
  101.9 10.2 %copy-start.5 = (bf16[32,264,132]{2,0,1:T(8,128)(2,1)}, bf16[32,264,132]{2,0,1:T(8,128)(2,1)S(1)}, u32[]{:S(2)}) copy-start(bf16[32,264,132]{2,0,1:T(8,128)(2,1)S(1)} %get-tuple-element.34) | copy-start | bytes 6690820
  101.9 10.2 %copy-start.13 = (bf16[32,32]{1,0:T(8,128)(2,1)S(1)}, bf16[32,32]{1,0:T(8,128)(2,1)}, u32[]{:S(2)}) copy-start(bf16[32,32]{1,0:T(8,128)(2,1)} %param.11) | copy-start | bytes 6148
  115.5 3.1 copy-start.3
  115.5 3.5 copy-start.7
  229.7 4.9 collective-permute-start.4
  232.5 7.2 %collective-permute-start.5 = (bf16[32,4,128]{2,0,1:T(8,128)(2,1)S(1)}, bf16[32,4,128]{2,0,1:T(8,128)(2,1)S(1)}, u32[]{:S(2)}, u32[]{:S(2)}) collective-permute-start(bf16[32,4,128]{2,0,1:T(8,128)(2,1)S(1)} %get-tuple-element.38), channel_id=1, source_target_pairs={{32,0},{64,32},{96,64},{128,96},{160,128},{192,160},{224,192},{256... | collective-permute-start | bytes 98312 | tf_op jit(solution)/shard_map/ppermute | solution.py:23
  251.8 10.8 %collective-permute-start.7 = (bf16[32,264,4]{1,0,2:T(8,128)(2,1)S(1)}, bf16[32,264,4]{1,0,2:T(8,128)(2,1)S(1)}, u32[]{:S(2)}, u32[]{:S(2)}) collective-permute-start(bf16[32,264,4]{1,0,2:T(8,128)(2,1)S(1)} %copy.26), channel_id=1, source_target_pairs={{0,1},{1,2},{2,3},{3,4},{4,5},{5,6},{6,7},{7,8},{8,9},{9,10},{10,1... | collective-permute-start | bytes 202760 | tf_op jit(solution)/shard_map/ppermute | solution.py:22
  253.7 5.8 collective-permute-start.6
  265.6 7.3 %copy-start.6 = (bf16[32,256,128]{2,0,1:T(8,128)(2,1)S(1)}, bf16[32,256,128]{2,0,1:T(8,128)(2,1)}, u32[]{:S(2)}) copy-start(bf16[32,256,128]{2,0,1:T(8,128)(2,1)} %get-tuple-element.50) | copy-start | bytes 6291460
  265.6 7.3 %copy-start.8 = (bf16[32,256,128]{2,0,1:T(8,128)(2,1)S(1)}, bf16[32,256,128]{2,0,1:T(8,128)(2,1)}, u32[]{:S(2)}) copy-start(bf16[32,256,128]{2,0,1:T(8,128)(2,1)} %multiply_convert_fusion.1) | copy-start | bytes 6291460
  272.9 109.6 %copy-start.9 = (bf16[256,512]{1,0:T(8,128)(2,1)S(1)}, bf16[256,512]{1,0:T(8,128)(2,1)}, u32[]{:S(2)}) copy-start(bf16[256,512]{1,0:T(8,128)(2,1)} %param.7) | copy-start | bytes 786436
  272.9 110.4 %copy-start.10 = (bf16[512,32]{0,1:T(8,128)(2,1)S(1)}, bf16[512,32]{0,1:T(8,128)(2,1)}, u32[]{:S(2)}) copy-start(bf16[512,32]{0,1:T(8,128)(2,1)} %param.8) | copy-start | bytes 98308
  272.9 227.5 %copy-start.11 = (bf16[512,32]{0,1:T(8,128)(2,1)S(1)}, bf16[512,32]{0,1:T(8,128)(2,1)}, u32[]{:S(2)}) copy-start(bf16[512,32]{0,1:T(8,128)(2,1)} %param.9) | copy-start | bytes 98308
Sparse Core Ops, SparseCore 0:
  500.5 165.3 all-reduce.3
where the time goes:
time: 675 us; the launch traced here: 674 us
  blocking collectives  365 us (54%)
  waiting for transfers between devices  176 us (26%)
  other arithmetic  39 us (6%)
  local copies, waits for them, and re-layouts  34 us (5%)
  matrix products  28.2 us (4%)
  starting transfers between devices  17 us (3%)
  between operations  14.4 us (2%)
    psum x1, waiting for transfers between devices, body(): wleft_sum, wright_sum = lax.psum((wleft_part, wright_part), 'row')  165 us
    psum x1, blocking collectives, body(): grad_left = lax.psum(left_part, 'col').astype(jnp.bfloat16)  102 us
    psum x1, blocking collectives, body(): lax.psum((kernel_part, point_part, head_part), ('row', 'col'))  96 us
    psum x1, blocking collectives, body(): column_total = lax.psum(right_part, 'row').astype(jnp.bfloat16)  80.7 us
    psum x1, blocking collectives, from_root(): return lax.psum(block, axis)  50.8 us
    all_gather x1, blocking collectives, body(): all_panels = lax.all_gather(column_total, 'col', axis=0, tiled=True)  35.4 us
    concatenate x4, other arithmetic, extended(): x = jnp.concatenate([before, x, after], axis=dim)  16.6 us
  transfers between devices with their start and end apart: 9, of which 5 were waited for; matrix products, arithmetic and copies ran while one was open for 2% of the time, Pallas kernels for 0%

commit v1 on v0

--- a/solution.py
+++ b/solution.py
@@ -135,7 +135,9 @@
     wright_part = lax.dot_general(
         bin_features, grad_right, contract, preferred_element_type=jnp.float32
     )
-    kernel_sum, point_sum, head_sum = lax.psum((kernel_part, point_part, head_part), ("row", "col"))
+    kernel_sum, point_sum, head_sum = lax.psum(
+        lax.psum((kernel_part, point_part, head_part), "row"), "col"
+    )
     wleft_sum, wright_sum = lax.psum((wleft_part, wright_part), "row")
     return (
         grad_features,

time: 675 us -> 572 us (0.85)
  blocking collectives: 365 us -> 269 us
    psum x2 -> x1, blocking collectives: 177 us -> 79.6 us  [body(): lax.psum((kernel_part, point_part, head_part), 'row')]
  transfers between devices with their start and end apart: 9 -> 9, of which waited for: 5 -> 4; matrix products, arithmetic and copies ran while one was open for 2% -> 3% of each run, Pallas kernels for 0% -> 0%
where the time goes in v1:
time: 572 us; the launch traced here: 571 us
  blocking collectives  269 us (47%)
  waiting for transfers between devices  172 us (30%)
  other arithmetic  38.8 us (7%)
  local copies, waits for them, and re-layouts  33.6 us (6%)
  matrix products  25 us (4%)
  starting transfers between devices  18.7 us (3%)
  between operations  14.4 us (3%)
    psum x1, waiting for transfers between devices, body(): wleft_sum, wright_sum = lax.psum((wleft_part, wright_part), 'row')  165 us
    psum x1, blocking collectives, body(): grad_left = lax.psum(left_part, 'col').astype(jnp.bfloat16)  103 us
    psum x1, blocking collectives, body(): lax.psum((kernel_part, point_part, head_part), 'row')  79.6 us
    psum x1, blocking collectives, from_root(): return lax.psum(block, axis)  50.8 us
    all_gather x1, blocking collectives, body(): all_panels = lax.all_gather(column_total, 'col', axis=0, tiled=True)  35.4 us
    concatenate x4, other arithmetic, extended(): x = jnp.concatenate([before, x, after], axis=dim)  16.8 us
  transfers between devices with their start and end apart: 9, of which 4 were waited for; matrix products, arithmetic and copies ran while one was open for 3% of the time, Pallas kernels for 0%

profile of v1, /device:TPU:8, one launch (start us, length us, event | category | flops | bytes accessed | tf_op | source)
XLA Modules:
  0.0 570.9 jit_solution(9039703027171774402)
XLA Ops:
  7.3 1.1 fusion.34
  8.4 50.8 %psum.77 = bf16[32,128]{1,0:T(8,128)(2,1)S(1)} all-reduce(bf16[32,128]{1,0:T(8,128)(2,1)S(1)} %fusion.34), channel_id=1, replica_groups=mesh['row'=16,'col'=32] {'row'}, use_global_device_ids=true, to_apply=%region_0.1 | all-reduce | flops 4096 | bytes 16384 | tf_op jit(solution)/shard_map/psum | solution.py:12
  59.2 1.1 fusion.29
  60.5 1.7 add_convert_fusion
  62.2 1.3 collective-permute-start
  63.5 1.3 collective-permute-start.1
  64.8 3.5 multiply_convert_fusion.1
  68.3 1.9 collective-permute-done.1
  70.2 0.3 pad_maximum_fusion.2
  70.5 2.9 fusion.51
  73.5 3.6 copy.20
  77.1 3.6 copy.22
  80.8 1.9 collective-permute-start.3
  82.7 2.6 collective-permute-start.2
  85.3 3.3 collective-permute-done.2
  88.6 3.0 copy.21
  91.6 3.0 copy.23
  94.7 7.2 %maximum_maximum_fusion = (bf16[32,264,132]{2,0,1:T(8,128)(2,1)S(1)}, bf16[32,264,132]{2,0,1:T(8,128)(2,1)S(1)}) fusion(bf16[32,4,128]{2,0,1:T(8,128)(2,1)S(1)} %collective-permute-done.1, bf16[32,256,128]{2,0,1:T(8,128)(2,1)} %copy-done.1, bf16[32,4,128]{2,0,1:T(8,128)(2,1)S(1)} %collective-permute-done, bf16[32,264,4]{2,0,1:T(8,128)(2,1)} %copy.21, ...), kind=kLoop, calls=%fused_computation.20 | loop fusion | flops 17842176 | bytes 6758400 | tf_op jit(solution)/shard_map/concatenate | solution.py:24
  101.9 9.8 %multiply_convert_fusion = (bf16[32,256,128]{2,0,1:T(8,128)(2,1)}, f32[32,256,128]{2,0,1:T(8,128)}) fusion(bf16[32,264,132]{2,0,1:T(8,128)(2,1)S(1)} %get-tuple-element.39, f32[32]{0:T(128)S(1)} %get-tuple-element.53, bf16[32,4,128]{2,0,1:T(8,128)(2,1)S(1)} %collective-permute-done.1, bf16[32,256,128]{2,0,1:T(8,128)(2,1)S(1)} %copy-done.2, ...), kind=kLoop, calls=%fused_computation.50 | loop fusion | flops 36700160 | bytes 21087360 | tf_op jit(solution)/shard_map/convert_element_type | solution.py:82
  111.7 10.2 %fusion.23 = (f32[32]{0:T(128)S(1)}, f32[32]{0:T(128)S(1)}, f32[32]{0:T(128)S(1)}, f32[32]{0:T(128)S(1)}, f32[32]{0:T(128)S(1)}, /*index=5*/f32[32]{0:T(128)S(1)...) fusion(bf16[32,264,132]{2,0,1:T(8,128)(2,1)S(1)} %get-tuple-element.39, ...), kind=kOutput, calls=%fused_computation.47 | convolution fusion | flops 110100192 | bytes 23186560 | tf_op jit(solution)/shard_map/co,oij->cij/dot_general | solution.py:77
  121.9 0.8 fusion.52
  122.6 4.5 collective-permute-start.4
  127.2 1.5 collective-permute-start.5
  128.7 3.4 fusion.30
  132.2 1.7 collective-permute-done.5
  133.9 1.9 pad_maximum_fusion.3
  135.8 2.9 fusion.50
  138.7 3.6 copy.24
  142.3 3.6 copy.26
  146.0 1.9 collective-permute-start.7
  147.9 3.6 collective-permute-start.6
  151.6 2.9 convolution_bitcast_fusion.2
  154.5 3.0 copy.25
  157.6 3.0 copy.27
  160.6 7.4 %pad_maximum_fusion.1 = (bf16[32,264,132]{2,0,1:T(8,128)(2,1)S(1)}, bf16[32,264,132]{2,0,1:T(8,128)(2,1)S(1)}) fusion(bf16[32,264,4]{2,0,1:T(8,128)(2,1)} %copy.25, bf16[32,4,128]{2,0,1:T(8,128)(2,1)S(1)} %collective-permute-done.5, bf16[32,256,128]{2,0,1:T(8,128)(2,1)} %get-tuple-element.55, bf16[32,4,128]{2,0,1:T(8,128)(2,1)S(1)} %collective-permute-done.4, ...), kind=kLoop, calls=%fused_computation.22 | loop fusion | flops 17842176 | bytes 6758400 | tf_op jit(solution)/shard_map/concatenate | solution.py:24
  168.1 7.2 %fusion.48 = (f32[32,128]{1,0:T(8,128)S(1)}, f32[32,256]{0,1:T(8,128)S(1)}) fusion(bf16[32,264,132]{2,0,1:T(8,128)(2,1)S(1)} %get-tuple-element.35, f32[32]{0:T(128)S(1)} %get-tuple-element.53, bf16[32,256,128]{2,0,1:T(8,128)(2,1)S(1)} %copy-done.3, bf16[32,4,128]{2,0,1:T(8,128)(2,1)S(1)} %collective-permute-done.4, f32[32]{0:T(128)S(1)} %get-tuple-element.54, ...), kind=kLoop, calls=%fused_computation.100 | loop fusion | flops 33542144 | bytes 16893056 | tf_op jit(solution)/shard_map/reduce_sum | solution.py:116
  175.3 79.6 %all-reduce.1 = (f32[9,32]{1,0:T(8,128)S(1)}, f32[32,32]{1,0:T(8,128)S(1)}, f32[32,24]{0,1:T(8,128)S(1)}, bf16[128,32]{0,1:T(8,128)(2,1)S(1)}) all-reduce(f32[9,32]{1,0:T(8,128)S(1)} %stack.39, f32[32,32]{1,0:T(8,128)S(1)} %convolution_bitcast_fusion.2, f32[32,24]{0,1:T(8,128)S(1)} %fusion.30, ...), channel_id=1, replica_groups=mesh['row'=16,'col'=32] {'row'}, use_global_device_ids=true, to_apply=%region_16.17 | all-reduce | flops 6176 | bytes 41216 | tf_op jit(solution)/shard_map/psum | solution.py:139
  254.9 102.7 %all-reduce = (bf16[256,32]{1,0:T(8,128)(2,1)S(1)}, f32[9,32]{1,0:T(8,128)S(1)}, f32[32,32]{1,0:T(8,128)S(1)}, f32[32,24]{0,1:T(8,128)S(1)}) all-reduce(f32[256,32]{1,0:T(8,128)S(1)} %bitcast.73, f32[9,32]{1,0:T(8,128)S(1)} %get-tuple-element.26, f32[32,32]{1,0:T(8,128)S(1)} %get-tuple-element.27, ...), channel_id=1, replica_groups=mesh['row'=16,'col'=32] {'col'}, use_global_device_ids=true, to_apply=%region_2.3 | all-reduce | flops 10272 | bytes 65792 | tf_op jit(solution)/shard_map/psum | solution.py:123
  357.6 0.8 convolution_bitcast_fusion.1
  358.5 0.2 fusion.54
  358.6 0.6 broadcast_multiply_fusion.3
  359.3 0.6 broadcast_multiply_fusion.2
  359.9 35.4 %all_gather.3 = bf16[4096,32]{0,1:T(8,128)(2,1)S(1)} all-gather(bf16[128,32]{0,1:T(8,128)(2,1)S(1)} %get-tuple-element.29), channel_id=1, replica_groups=mesh['row'=16,'col'=32] {'col'}, dimensions={0}, use_global_device_ids=true | all-gather | bytes 270336 | tf_op jit(solution)/shard_map/all_gather | solution.py:125
  395.3 0.8 convolution_bitcast_fusion
  396.1 1.0 fusion.28
  397.1 0.6 broadcast_multiply_fusion.4
  397.7 164.8 %all-reduce.5.cloned.1.call-done = (f32[512,32]{0,1:T(8,128)}, f32[512,32]{0,1:T(8,128)}) async-done(((f32[512,32]{0,1:T(8,128)}, f32[512,32]{0,1:T(8,128)}), (f32[512,32]{0,1:T(8,128)}, f32[512,32]{0,1:T(8,128)})) %all-reduce.5.cloned.1.call-update) | async-done | bytes 131088 | tf_op jit(solution)/shard_map/psum | solution.py:141
  562.5 1.5 broadcast_multiply_fusion
  (32 shorter events, 0.3 us)
Async XLA Ops:
  7.2 57.7 %copy-start = (bf16[24,256,128]{2,1,0:T(8,128)(2,1)S(1)}, bf16[24,256,128]{2,1,0:T(8,128)(2,1)}, u32[]{:S(2)}) copy-start(bf16[24,256,128]{2,1,0:T(8,128)(2,1)} %param.13) | copy-start | bytes 4718596
  7.2 555.3 %all-reduce.5.cloned.1.call-start = ((), (), s32[]{:S(2)}) async-start(), calls=%async_computation | async-start | bytes 262144 | tf_op jit(solution)/shard_map/psum | solution.py:141
  62.2 8.0 %copy-start.1 = (bf16[32,256,128]{2,0,1:T(8,128)(2,1)}, bf16[32,256,128]{2,0,1:T(8,128)(2,1)S(1)}, u32[]{:S(2)}) copy-start(bf16[32,256,128]{2,0,1:T(8,128)(2,1)S(1)} %add_convert_fusion) | copy-start | bytes 6291460
  62.2 6.1 %collective-permute-start = (bf16[32,4,128]{2,0,1:T(8,128)(2,1)S(1)}, bf16[32,4,128]{2,0,1:T(8,128)(2,1)S(1)}, u32[]{:S(2)}, u32[]{:S(2)}) collective-permute-start(bf16[32,4,128]{2,0,1:T(8,128)(2,1)S(1)} %get-tuple-element.44), channel_id=1, source_target_pairs={{0,32},{32,64},{64,96},{96,128},{128,160},{160,192},{192,224},{224... | collective-permute-start | bytes 98312 | tf_op jit(solution)/shard_map/ppermute | solution.py:22
  63.5 6.7 %collective-permute-start.1 = (bf16[32,4,128]{2,0,1:T(8,128)(2,1)S(1)}, bf16[32,4,128]{2,0,1:T(8,128)(2,1)S(1)}, u32[]{:S(2)}, u32[]{:S(2)}) collective-permute-start(bf16[32,4,128]{2,0,1:T(8,128)(2,1)S(1)} %get-tuple-element.45), channel_id=1, source_target_pairs={{32,0},{64,32},{96,64},{128,96},{160,128},{192,160},{224,192},{256... | collective-permute-start | bytes 98312 | tf_op jit(solution)/shard_map/ppermute | solution.py:23
  73.5 11.8 %copy-start.8 = (f32[9,32]{1,0:T(8,128)S(1)}, f32[9,32]{1,0:T(8,128)}, u32[]{:S(2)}) copy-start(f32[9,32]{1,0:T(8,128)} %param.10) | copy-start | bytes 3460
  80.8 10.9 %collective-permute-start.3 = (bf16[32,264,4]{1,0,2:T(8,128)(2,1)S(1)}, bf16[32,264,4]{1,0,2:T(8,128)(2,1)S(1)}, u32[]{:S(2)}, u32[]{:S(2)}) collective-permute-start(bf16[32,264,4]{1,0,2:T(8,128)(2,1)S(1)} %copy.22), channel_id=1, source_target_pairs={{1,0},{2,1},{3,2},{4,3},{5,4},{6,5},{7,6},{8,7},{9,8},{10,9},{11,1... | collective-permute-start | bytes 202760 | tf_op jit(solution)/shard_map/ppermute | solution.py:23
  82.7 5.9 %collective-permute-start.2 = (bf16[32,264,4]{1,0,2:T(8,128)(2,1)S(1)}, bf16[32,264,4]{1,0,2:T(8,128)(2,1)S(1)}, u32[]{:S(2)}, u32[]{:S(2)}) collective-permute-start(bf16[32,264,4]{1,0,2:T(8,128)(2,1)S(1)} %copy.20), channel_id=1, source_target_pairs={{0,1},{1,2},{2,3},{3,4},{4,5},{5,6},{6,7},{7,8},{8,9},{9,10},{10,1... | collective-permute-start | bytes 202760 | tf_op jit(solution)/shard_map/ppermute | solution.py:22
  94.7 7.2 %copy-start.2 = (bf16[32,256,128]{2,0,1:T(8,128)(2,1)S(1)}, bf16[32,256,128]{2,0,1:T(8,128)(2,1)}, u32[]{:S(2)}) copy-start(bf16[32,256,128]{2,0,1:T(8,128)(2,1)} %copy-done.1) | copy-start | bytes 6291460
  101.9 9.8 %copy-start.9 = (bf16[32,32]{1,0:T(8,128)(2,1)S(1)}, bf16[32,32]{1,0:T(8,128)(2,1)}, u32[]{:S(2)}) copy-start(bf16[32,32]{1,0:T(8,128)(2,1)} %param.11) | copy-start | bytes 6148
  122.6 9.5 %collective-permute-start.4 = (bf16[32,4,128]{2,0,1:T(8,128)(2,1)S(1)}, bf16[32,4,128]{2,0,1:T(8,128)(2,1)S(1)}, u32[]{:S(2)}, u32[]{:S(2)}) collective-permute-start(bf16[32,4,128]{2,0,1:T(8,128)(2,1)S(1)} %get-tuple-element.42), channel_id=1, source_target_pairs={{0,32},{32,64},{64,96},{96,128},{128,160},{160,192},{192,224},{224... | collective-permute-start | bytes 98312 | tf_op jit(solution)/shard_map/ppermute | solution.py:22
  127.2 6.7 %collective-permute-start.5 = (bf16[32,4,128]{2,0,1:T(8,128)(2,1)S(1)}, bf16[32,4,128]{2,0,1:T(8,128)(2,1)S(1)}, u32[]{:S(2)}, u32[]{:S(2)}) collective-permute-start(bf16[32,4,128]{2,0,1:T(8,128)(2,1)S(1)} %get-tuple-element.43), channel_id=1, source_target_pairs={{32,0},{64,32},{96,64},{128,96},{160,128},{192,160},{224,192},{256... | collective-permute-start | bytes 98312 | tf_op jit(solution)/shard_map/ppermute | solution.py:23
  146.0 11.6 %collective-permute-start.7 = (bf16[32,264,4]{1,0,2:T(8,128)(2,1)S(1)}, bf16[32,264,4]{1,0,2:T(8,128)(2,1)S(1)}, u32[]{:S(2)}, u32[]{:S(2)}) collective-permute-start(bf16[32,264,4]{1,0,2:T(8,128)(2,1)S(1)} %copy.26), channel_id=1, source_target_pairs={{0,1},{1,2},{2,3},{3,4},{4,5},{5,6},{6,7},{7,8},{8,9},{9,10},{10,1... | collective-permute-start | bytes 202760 | tf_op jit(solution)/shard_map/ppermute | solution.py:22
  147.9 6.6 %collective-permute-start.6 = (bf16[32,264,4]{1,0,2:T(8,128)(2,1)S(1)}, bf16[32,264,4]{1,0,2:T(8,128)(2,1)S(1)}, u32[]{:S(2)}, u32[]{:S(2)}) collective-permute-start(bf16[32,264,4]{1,0,2:T(8,128)(2,1)S(1)} %copy.24), channel_id=1, source_target_pairs={{1,0},{2,1},{3,2},{4,3},{5,4},{6,5},{7,6},{8,7},{9,8},{10,9},{11,1... | collective-permute-start | bytes 202760 | tf_op jit(solution)/shard_map/ppermute | solution.py:23
  160.6 7.4 %copy-start.3 = (bf16[32,256,128]{2,0,1:T(8,128)(2,1)S(1)}, bf16[32,256,128]{2,0,1:T(8,128)(2,1)}, u32[]{:S(2)}) copy-start(bf16[32,256,128]{2,0,1:T(8,128)(2,1)} %get-tuple-element.55) | copy-start | bytes 6291460
  160.6 7.4 %copy-start.4 = (bf16[32,256,128]{2,0,1:T(8,128)(2,1)S(1)}, bf16[32,256,128]{2,0,1:T(8,128)(2,1)}, u32[]{:S(2)}) copy-start(bf16[32,256,128]{2,0,1:T(8,128)(2,1)} %multiply_convert_fusion.1) | copy-start | bytes 6291460
  168.0 189.6 %copy-start.5 = (bf16[256,512]{1,0:T(8,128)(2,1)S(1)}, bf16[256,512]{1,0:T(8,128)(2,1)}, u32[]{:S(2)}) copy-start(bf16[256,512]{1,0:T(8,128)(2,1)} %param.7) | copy-start | bytes 786436
  168.1 190.4 %copy-start.6 = (bf16[512,32]{0,1:T(8,128)(2,1)S(1)}, bf16[512,32]{0,1:T(8,128)(2,1)}, u32[]{:S(2)}) copy-start(bf16[512,32]{0,1:T(8,128)(2,1)} %param.8) | copy-start | bytes 98308
  168.1 228.0 %copy-start.7 = (bf16[512,32]{0,1:T(8,128)(2,1)S(1)}, bf16[512,32]{0,1:T(8,128)(2,1)}, u32[]{:S(2)}) copy-start(bf16[512,32]{0,1:T(8,128)(2,1)} %param.9) | copy-start | bytes 98308
Sparse Core Ops, SparseCore 0:
  397.2 165.2 all-reduce.4
